TPU v7x, 32 devices: a whole 2x2x4 slice. The times are simulated.
32 devices in a mesh: slab: 8 (over z, x), grp: 4 (over y, core).
Axes of the slice: x: 2, y: 2, z: 4, core: 2. Of those that a mesh axis runs over, the one named last changes fastest.
Arguments:
- iterate: float32 [3072, 256], P(('slab', 'grp')), may hold values from -6 to 6
- residual: float32 [3072, 256], P(('slab', 'grp')), may hold values from -6 to 6
- direction: float32 [3072, 256], P(('slab', 'grp')), may hold values from -6 to 6
- prior_rho: float32 [256], replicated, may hold values from 1536 to 6144
- diag_blocks: float32 [3072, 384], P(('slab', 'grp')), as said below
- lower_coupling: float32 [3072, 128], P(('slab', 'grp')), may hold values from -0.125 to 0.125
- upper_coupling: float32 [3072, 128], P(('slab', 'grp')), may hold values from -0.125 to 0.125
- interface: int32 [8, 128], P('slab'), may hold values from 0 to 383, as said below
- jacobi_inverse: float32 [3072, 96], P(('slab', 'grp'))
- slab_inverse: float32 [3072, 384], P(('slab', 'grp'))
- lower_factor: float32 [3072, 128], P(('slab', 'grp')), may hold values from -0.875 to 0.875
- upper_factor: float32 [3072, 128], P(('slab', 'grp')), may hold values from -0.5 to 0.5
Outputs:
- new_iterate: float32 [3072, 256], P(('slab', 'grp'))
- new_residual: float32 [3072, 256], P(('slab', 'grp'))
- new_direction: float32 [3072, 256], P(('slab', 'grp'))
- new_rho: float32 [256], replicated
Inputs may be any that keep to these rules, and one draw needn't show every extreme that they name: `interface`: row k lists 128 distinct dof numbers of slab k. `diag_blocks`: each diagonal block is a positive diagonal plus a skew-symmetric part.
All inputs are finite; a program needn't handle non-finite values.
Results may differ from a plain program's by a relative error of at most 0.0003.
Values sent between devices are 32-bit elements; how exact they have to be, the bound alone decides.
A program may use at most 64 MiB of HBM per device.

v0:
```python
import jax
import jax.numpy as jnp
from jax import lax
from jax.sharding import PartitionSpec as P


def extended(cells, sides, width):
    for axis, dim in sides:
        count = lax.axis_size(axis)
        ends = count - 1
        head = lax.slice_in_dim(cells, 0, width, axis=dim)
        tail = lax.slice_in_dim(cells, cells.shape[dim] - width, cells.shape[dim], axis=dim)
        cells = jnp.concatenate(
            [
                lax.ppermute(tail, axis, [(i, (i + 1) % count) for i in range(ends)]),
                cells,
                lax.ppermute(head, axis, [((i + 1) % count, i) for i in range(ends)]),
            ],
            axis=dim,
        )
    return cells


def prefix(part, axis, combine, identity, reverse):
    count = lax.axis_size(axis)
    place = lax.axis_index(axis)
    ahead = count - 1 - place if reverse else place
    gathered = jax.tree.map(lambda a: lax.all_gather(a, axis), part)
    state = jax.tree.map(lambda a, e: jnp.zeros_like(a) + jnp.asarray(e, a.dtype), part, identity)

    def one(turn, state):
        source = count - 1 - turn if reverse else turn
        return combine(
            state, jax.tree.map(lambda a: lax.dynamic_index_in_dim(a, source, 0, False), gathered)
        )

    return lax.fori_loop(0, ahead, one, state)


def matmul(left, right):
    return jnp.dot(left, right, precision=lax.Precision.HIGHEST, preferred_element_type=jnp.float32)


def compose(earlier, later):
    return (matmul(later[0], earlier[0]), matmul(later[0], earlier[1]) + later[1])


def local(
    iterate,
    residual,
    direction,
    prior_rho,
    diag_blocks,
    lower_coupling,
    upper_coupling,
    interface,
    jacobi_inverse,
    slab_inverse,
    lower_factor,
    upper_factor,
):
    index_rows = interface[0]

    def operate(field):
        gathered = lax.all_gather(field, "grp", axis=0, tiled=True)
        faces = gathered[index_rows]
        beside_all = extended(faces[None], (("slab", 0),), 1)
        return (
            matmul(diag_blocks, gathered)
            + matmul(lower_coupling, beside_all[0])
            + matmul(upper_coupling, beside_all[2])
        )

    image = operate(direction)
    curvature = lax.psum(jnp.sum(direction * image, axis=0), ("slab", "grp"))
    step_size = prior_rho / curvature
    new_iterate = iterate + step_size * direction
    new_residual = residual - step_size * image
    smoothed = matmul(jacobi_inverse, new_residual)
    defect = new_residual - operate(smoothed)
    defect_full, lower_full, upper_full = (
        lax.all_gather(defect, "grp", axis=0, tiled=True),
        lax.all_gather(lower_factor, "grp", axis=0, tiled=True),
        lax.all_gather(upper_factor, "grp", axis=0, tiled=True),
    )
    solved = matmul(slab_inverse, defect_full)
    factor_rows = matmul(slab_inverse, lower_full)
    solved_full, factor_full = (
        lax.all_gather(solved, "grp", axis=0, tiled=True),
        lax.all_gather(factor_rows, "grp", axis=0, tiled=True),
    )
    offsets = solved_full[index_rows]
    transfer = -factor_full[index_rows]
    upper_iface = -upper_full[index_rows]
    identity_map = jnp.eye(transfer.shape[0], dtype=jnp.float32)
    forward_map = prefix(
        (transfer, offsets), "slab", compose, (identity_map, jnp.zeros_like(offsets)), False
    )
    forward_prev = forward_map[1]
    forward_vals = solved - matmul(factor_rows, forward_prev)
    iface_vals = offsets + matmul(transfer, forward_prev)
    backward_map = prefix(
        (upper_iface, iface_vals), "slab", compose, (identity_map, jnp.zeros_like(iface_vals)), True
    )
    backward_next = backward_map[1]
    correction = forward_vals - matmul(upper_factor, backward_next)
    precond = smoothed + correction
    new_rho = lax.psum(jnp.sum(new_residual * precond, axis=0), ("slab", "grp"))
    new_direction = precond + new_rho / prior_rho * direction
    return (new_iterate, new_residual, new_direction, new_rho)


def solution(mesh):
    in_specs = (
        P(("slab", "grp"), None),
        P(("slab", "grp"), None),
        P(("slab", "grp"), None),
        P(),
        P(("slab", "grp"), None),
        P(("slab", "grp"), None),
        P(("slab", "grp"), None),
        P("slab", None),
        P(("slab", "grp"), None),
        P(("slab", "grp"), None),
        P(("slab", "grp"), None),
        P(("slab", "grp"), None),
    )
    out_specs = (P(("slab", "grp"), None), P(("slab", "grp"), None), P(("slab", "grp"), None), P())
    return jax.shard_map(local, mesh=mesh, in_specs=in_specs, out_specs=out_specs, check_vma=False)
```

profile of v0, /device:TPU:0, one launch (start us, length us, event | category | flops | bytes accessed | tf_op | source)
XLA Modules:
  0.0 253.6 jit_solution(16513600514509766951)
XLA Ops:
  7.2 0.0 copy-start
  7.2 0.0 all-gather.7.cloned.1.call-start
  7.2 0.7 fusion.16
  7.9 8.2 %all_gather.41 = f32[384,256]{1,0:T(8,128)S(1)} all-gather(f32[96,256]{1,0:T(8,128)} %param.18), channel_id=1, replica_groups=mesh['slab'=8,'grp'=4] {'grp'}, dimensions={0}, use_global_device_ids=true | all-gather | bytes 491520 | tf_op jit(solution)/shard_map/all_gather | solution.py:65
  16.1 0.8 gather_fusion
  16.8 0.0 copy-start.7
  16.9 3.5 %collective-permute-start = (f32[1,128,256]{2,1,0:T(8,128)S(1)}, f32[1,128,256]{2,1,0:T(8,128)S(1)}, u32[]{:S(2)}, u32[]{:S(2)}) collective-permute-start(f32[1,128,256]{2,1,0:T(8,128)S(1)} %bitcast.93), channel_id=1, source_target_pairs={{0,4},{4,8},{8,12},{12,16},{16,20},{20,24},{24,28},{1,5},{5,9},{9,... | collective-permute-start | bytes 393224 | tf_op jit(solution)/shard_map/ppermute | solution.py:15
  20.4 1.3 collective-permute-start.1
  21.7 0.4 fusion.18
  22.1 0.0 copy-start.3
  22.1 0.0 copy-start.5
  22.1 1.5 collective-permute-done
  23.6 0.2 fusion.9
  23.9 0.0 copy-start.8
  23.9 3.9 %collective-permute-done.1 = f32[1,128,256]{2,1,0:T(8,128)S(1)} collective-permute-done((f32[1,128,256]{2,1,0:T(8,128)S(1)}, f32[1,128,256]{2,1,0:T(8,128)S(1)}, u32[]{:S(2)}, u32[]{:S(2)}) %collective-permute-start.1) | collective-permute-done | bytes 131104 | tf_op jit(solution)/shard_map/ppermute | solution.py:17
  27.8 0.3 multiply_reduce_fusion.1
  28.0 0.0 copy-start.12
  28.0 41.1 %psum.14 = f32[256]{0:T(256)S(1)} all-reduce(f32[256]{0:T(256)S(1)} %get-tuple-element.156), channel_id=1, replica_groups=mesh['slab'=8,'grp'=4] {'slab','grp'}, use_global_device_ids=true, to_apply=%region_1.0 | all-reduce | flops 256 | bytes 2048 | tf_op jit(solution)/shard_map/psum | solution.py:75
  69.1 0.0 copy-start.10
  69.2 0.8 copy-done.10
  70.0 0.2 convolution_bitcast_fusion.1
  70.2 7.2 %all_gather.42 = f32[384,256]{1,0:T(8,128)S(1)} all-gather(f32[96,256]{1,0:T(8,128)S(1)} %convolution_bitcast_fusion.1), channel_id=1, replica_groups=mesh['slab'=8,'grp'=4] {'grp'}, dimensions={0}, use_global_device_ids=true | all-gather | bytes 491520 | tf_op jit(solution)/shard_map/all_gather | solution.py:65
  77.4 0.8 gather_fusion.1
  78.2 3.1 %collective-permute-start.2 = (f32[1,128,256]{2,1,0:T(8,128)S(1)}, f32[1,128,256]{2,1,0:T(8,128)S(1)}, u32[]{:S(2)}, u32[]{:S(2)}) collective-permute-start(f32[1,128,256]{2,1,0:T(8,128)S(1)} %bitcast.95), channel_id=1, source_target_pairs={{0,4},{4,8},{8,12},{12,16},{16,20},{20,24},{24,28},{1,5},{5,9},{9,... | collective-permute-start | bytes 393224 | tf_op jit(solution)/shard_map/ppermute | solution.py:15
  81.3 1.3 collective-permute-start.3
  82.6 0.4 fusion.19
  83.0 1.6 collective-permute-done.2
  84.5 0.2 convolution_add_fusion.4
  84.8 3.9 %collective-permute-done.3 = f32[1,128,256]{2,1,0:T(8,128)S(1)} collective-permute-done((f32[1,128,256]{2,1,0:T(8,128)S(1)}, f32[1,128,256]{2,1,0:T(8,128)S(1)}, u32[]{:S(2)}, u32[]{:S(2)}) %collective-permute-start.3) | collective-permute-done | bytes 131104 | tf_op jit(solution)/shard_map/ppermute | solution.py:17
  88.7 0.2 fusion.10
  88.9 0.0 copy-start.4
  88.9 6.3 %all_gather.43 = f32[384,256]{1,0:T(8,128)S(1)} all-gather(f32[96,256]{1,0:T(8,128)S(1)} %fusion.10), channel_id=1, replica_groups=mesh['slab'=8,'grp'=4] {'grp'}, dimensions={0}, use_global_device_ids=true | all-gather | bytes 491520 | tf_op jit(solution)/shard_map/all_gather | solution.py:82
  95.2 0.4 convolution_bitcast_fusion.4
  95.6 6.6 %all_gather.47 = f32[384,256]{1,0:T(8,128)S(1)} all-gather(f32[96,256]{1,0:T(8,128)S(1)} %convolution_bitcast_fusion.4), channel_id=1, replica_groups=mesh['slab'=8,'grp'=4] {'grp'}, dimensions={0}, use_global_device_ids=true | all-gather | bytes 491520 | tf_op jit(solution)/shard_map/all_gather | solution.py:89
  102.1 1.4 gather_fusion.3
  103.5 0.0 all-gather.7.cloned.1.call-update
  103.6 0.0 all-gather.9.cloned.1.call-start
  103.6 0.7 copy-done.11
  104.3 5.6 %all_gather.44 = f32[384,128]{1,0:T(8,128)S(1)} all-gather(f32[96,128]{1,0:T(8,128)S(1)} %copy-done.11), channel_id=1, replica_groups=mesh['slab'=8,'grp'=4] {'grp'}, dimensions={0}, use_global_device_ids=true | all-gather | bytes 245760 | tf_op jit(solution)/shard_map/all_gather | solution.py:83
  109.9 0.3 fusion.20
  110.2 5.6 %all_gather.45 = f32[384,128]{1,0:T(8,128)S(1)} all-gather(f32[96,128]{1,0:T(8,128)S(1)} %fusion.20), channel_id=1, replica_groups=mesh['slab'=8,'grp'=4] {'grp'}, dimensions={0}, use_global_device_ids=true | all-gather | bytes 245760 | tf_op jit(solution)/shard_map/all_gather | solution.py:90
  115.8 0.6 gather_fusion.2
  116.5 32.3 %all-gather = f32[1024,128]{1,0:T(8,128)S(1)} all-gather(f32[128,128]{1,0:T(8,128)S(1)} %neg.26), channel_id=2, replica_groups=mesh['slab'=8,'grp'=4] {'slab'}, dimensions={0}, use_global_device_ids=true | all-gather | bytes 589824 | tf_op jit(solution)/shard_map/all_gather | solution.py:28
  148.8 0.9 copy-done.2
  149.7 0.9 convolution_add_fusion.2
  150.6 0.0 all-gather.9.cloned.1.call-update
  150.6 0.8 copy-done.6
  151.4 5.6 %all_gather.50 = f32[384,128]{1,0:T(8,128)S(1)} all-gather(f32[96,128]{1,0:T(8,128)S(1)} %copy-done.6), channel_id=1, replica_groups=mesh['slab'=8,'grp'=4] {'grp'}, dimensions={0}, use_global_device_ids=true | all-gather | bytes 245760 | tf_op jit(solution)/shard_map/all_gather | solution.py:84
  157.0 0.6 gather_fusion.4
  157.6 37.4 %all-gather.2 = f32[1024,128]{1,0:T(8,128)S(1)} all-gather(f32[128,128]{1,0:T(8,128)S(1)} %neg.28), channel_id=4, replica_groups=mesh['slab'=8,'grp'=4] {'slab'}, dimensions={0}, use_global_device_ids=true | all-gather | bytes 589824 | tf_op jit(solution)/shard_map/all_gather | solution.py:28
  195.0 0.2 convolution_subtract_fusion
  195.2 4.5 %all-gather.9.cloned.1.call-done = f32[1024,256]{1,0:T(8,128)} async-done(((f32[128,256]{1,0:T(8,128)}), f32[1024,256]{1,0:T(8,128)}) %all-gather.9.cloned.1.call-update) | async-done | bytes 1048592 | tf_op jit(solution)/shard_map/all_gather | solution.py:28
  199.8 8.6 %while.27 = (s32[]{:T(128)}, f32[128,256]{1,0:T(8,128)S(1)}, s32[]{:T(128)}, f32[8,128,128]{2,1,0:T(8,128)S(1)}, f32[8,128,256]{2,1,0:T(8,128)}, /*index=5*/s32[]{:T(128)}, s32[]{:T(128)}, s32[]{:T(128)}, s32[]{:T(128)}) while((s32[]{:T(128)}, f32[128,256]{1,0:T(8,128)S(1)}, s32[]{:T(128)}, f32[8,128,128]{2,1,0:T(8,128)S(1)}, ...), condition=%wide.region_5.6_spmd, body=%wide.region_4.5_spmd.sunk | while | flops 50364420 | bytes 722059 | solution.py:37
  199.8 1.2 convolution_add_fusion.8
  201.0 1.2 convolution_add_fusion.8
  202.2 1.2 convolution_add_fusion.8
  203.5 1.2 convolution_add_fusion.8
  204.7 1.2 convolution_add_fusion.8
  205.9 1.2 convolution_add_fusion.8
  207.1 1.2 convolution_add_fusion.8
  208.3 0.3 multiply_reduce_fusion
  208.6 36.9 %psum.15 = f32[256]{0:T(256)S(1)} all-reduce(f32[256]{0:T(256)S(1)} %get-tuple-element.158), channel_id=1, replica_groups=mesh['slab'=8,'grp'=4] {'slab','grp'}, use_global_device_ids=true, to_apply=%region_7.8 | all-reduce | flops 256 | bytes 2048 | tf_op jit(solution)/shard_map/psum | solution.py:108
  245.5 0.6 copy-done.13
  246.0 0.7 multiply_add_fusion
  (32 shorter events, 0.2 us)
Async XLA Ops:
  7.2 14.5 %copy-start = (f32[96,384]{1,0:T(8,128)S(1)}, f32[96,384]{1,0:T(8,128)}, u32[]{:S(2)}) copy-start(f32[96,384]{1,0:T(8,128)} %param.20) | copy-start | bytes 442372
  7.2 141.6 %all-gather.7.cloned.1.call-start = ((), (), s32[]{:S(2)}) async-start(), calls=%async_computation | async-start | bytes 1179648 | tf_op jit(solution)/shard_map/all_gather | solution.py:28
  16.8 6.8 %copy-start.7 = (f32[96,128]{1,0:T(8,128)S(1)}, f32[96,128]{1,0:T(8,128)}, u32[]{:S(2)}) copy-start(f32[96,128]{1,0:T(8,128)} %param.21) | copy-start | bytes 147460
  16.9 6.8 %collective-permute-start = (f32[1,128,256]{2,1,0:T(8,128)S(1)}, f32[1,128,256]{2,1,0:T(8,128)S(1)}, u32[]{:S(2)}, u32[]{:S(2)}) collective-permute-start(f32[1,128,256]{2,1,0:T(8,128)S(1)} %bitcast.93), channel_id=1, source_target_pairs={{0,4},{4,8},{8,12},{12,16},{16,20},{20,24},{24,28},{1,5},{5,9},{9,... | collective-permute-start | bytes 393224 | tf_op jit(solution)/shard_map/ppermute | solution.py:15
  20.4 7.4 %collective-permute-start.1 = (f32[1,128,256]{2,1,0:T(8,128)S(1)}, f32[1,128,256]{2,1,0:T(8,128)S(1)}, u32[]{:S(2)}, u32[]{:S(2)}) collective-permute-start(f32[1,128,256]{2,1,0:T(8,128)S(1)} %bitcast.94), channel_id=1, source_target_pairs={{4,0},{8,4},{12,8},{16,12},{20,16},{24,20},{28,24},{5,1},{9,5},{13... | collective-permute-start | bytes 393224 | tf_op jit(solution)/shard_map/ppermute | solution.py:17
  22.1 5.7 %copy-start.3 = (f32[96,256]{1,0:T(8,128)S(1)}, f32[96,256]{1,0:T(8,128)}, u32[]{:S(2)}) copy-start(f32[96,256]{1,0:T(8,128)} %param.18) | copy-start | bytes 294916
  22.1 5.7 %copy-start.5 = (f32[96,128]{1,0:T(8,128)S(1)}, f32[96,128]{1,0:T(8,128)}, u32[]{:S(2)}) copy-start(f32[96,128]{1,0:T(8,128)} %param.22) | copy-start | bytes 147460
  23.9 45.3 %copy-start.8 = (f32[96,256]{1,0:T(8,128)S(1)}, f32[96,256]{1,0:T(8,128)}, u32[]{:S(2)}) copy-start(f32[96,256]{1,0:T(8,128)} %param.17) | copy-start | bytes 294916
  28.0 41.1 %copy-start.12 = (f32[256]{0:T(256)S(1)}, f32[256]{0:T(256)}, u32[]{:S(2)}) copy-start(f32[256]{0:T(256)} %param.19) | copy-start | bytes 3076
  69.1 0.8 copy-start.10
  70.0 138.4 %copy-start.1 = (f32[96,256]{1,0:T(8,128)}, f32[96,256]{1,0:T(8,128)S(1)}, u32[]{:S(2)}) copy-start(f32[96,256]{1,0:T(8,128)S(1)} %multiply_subtract_fusion) | copy-start | bytes 294916
  78.2 6.3 %collective-permute-start.2 = (f32[1,128,256]{2,1,0:T(8,128)S(1)}, f32[1,128,256]{2,1,0:T(8,128)S(1)}, u32[]{:S(2)}, u32[]{:S(2)}) collective-permute-start(f32[1,128,256]{2,1,0:T(8,128)S(1)} %bitcast.95), channel_id=1, source_target_pairs={{0,4},{4,8},{8,12},{12,16},{16,20},{20,24},{24,28},{1,5},{5,9},{9,... | collective-permute-start | bytes 393224 | tf_op jit(solution)/shard_map/ppermute | solution.py:15
  81.3 7.4 %collective-permute-start.3 = (f32[1,128,256]{2,1,0:T(8,128)S(1)}, f32[1,128,256]{2,1,0:T(8,128)S(1)}, u32[]{:S(2)}, u32[]{:S(2)}) collective-permute-start(f32[1,128,256]{2,1,0:T(8,128)S(1)} %bitcast.96), channel_id=1, source_target_pairs={{4,0},{8,4},{12,8},{16,12},{20,16},{24,20},{28,24},{5,1},{9,5},{13... | collective-permute-start | bytes 393224 | tf_op jit(solution)/shard_map/ppermute | solution.py:17
  88.9 6.3 %copy-start.4 = (f32[96,384]{1,0:T(8,128)S(1)}, f32[96,384]{1,0:T(8,128)}, u32[]{:S(2)}) copy-start(f32[96,384]{1,0:T(8,128)} %param.25) | copy-start | bytes 442372
  103.5 0.8 copy-start.11
  103.6 96.2 %all-gather.9.cloned.1.call-start = ((), (), s32[]{:S(2)}) async-start(), calls=%async_computation.1 | async-start | bytes 1179648 | tf_op jit(solution)/shard_map/all_gather | solution.py:28
  148.8 0.9 copy-start.2
  150.6 0.8 copy-start.6
  208.3 37.7 %copy-start.9 = (f32[96,256]{1,0:T(8,128)S(1)}, f32[96,256]{1,0:T(8,128)}, u32[]{:S(2)}) copy-start(f32[96,256]{1,0:T(8,128)} %param.16) | copy-start | bytes 294916
  245.5 0.6 copy-start.13
Sparse Core Ops, SparseCore 0:
  103.7 42.9 all-gather.6
  150.7 48.9 all-gather.8
where the time goes:
time: 255 us; the launch traced here: 254 us
  blocking collectives  193 us (76%)
  waiting for transfers between devices  15.4 us (6%)
  between operations  14.3 us (6%)
  matrix products  12.2 us (5%)
  starting transfers between devices  9.29 us (4%)
  local copies, waits for them, and re-layouts  8.05 us (3%)
    all_gather x2, blocking collectives, prefix(): gathered = jax.tree.map(lambda a: lax.all_gather(a, axis), part)  69.6 us
    psum x1, blocking collectives, local(): curvature = lax.psum(jnp.sum(direction * image, axis=0), ('slab', 'grp'))  41.1 us
    psum x1, blocking collectives, local(): new_rho = lax.psum(jnp.sum(new_residual * precond, axis=0), ('slab', 'grp'))  36.9 us
    all_gather x2, blocking collectives, operate(): gathered = lax.all_gather(field, 'grp', axis=0, tiled=True)  15.4 us
    dot_general x19, matrix products, matmul(): jnp.dot(left, right, precision=lax.Precision.HIGHEST, preferred_element_t...  12.2 us
    ppermute x2, waiting for transfers between devices, extended(): lax.ppermute(head, axis, [((i + 1) % count, i) for i in range(ends)])  7.72 us
    ppermute x2, starting transfers between devices, extended(): lax.ppermute(tail, axis, [(i, (i + 1) % count) for i in range(ends)])  6.62 us
    all_gather x1, blocking collectives, local(): lax.all_gather(solved, 'grp', axis=0, tiled=True)  6.57 us
  transfers between devices with their start and end apart: 6, of which 5 were waited for; matrix products, arithmetic and copies ran while one was open for 1% of the time, Pallas kernels for 0%

commit v1 on v0

v1 whole, which is shorter than its diff:
```python
import functools

import jax
import jax.numpy as jnp
from jax import lax
from jax.experimental import pallas as pl
from jax.experimental.pallas import tpu as pltpu
from jax.sharding import PartitionSpec as P

MESH = pl.DeviceIdType.MESH
BF = jnp.bfloat16
F32 = jnp.float32
LANES = 128


def split(x):
    hi = x.astype(BF)
    return hi, (x - hi.astype(F32)).astype(BF)


def dot(a, b):
    return jnp.dot(a, b, preferred_element_type=F32)


def mm(ah, al, b):
    bh, bl = split(b)
    width = b.shape[1]
    both = dot(ah, jnp.concatenate([bh, bl], axis=1))
    return both[:, :width] + (both[:, width:] + dot(al, bh))


def pick(sel, b):
    bh, bl = split(b)
    width = b.shape[1]
    both = dot(sel, jnp.concatenate([bh, bl], axis=1))
    return both[:, :width] + both[:, width:]


def each(low, high, fn):
    if high - low <= 16:
        for i in range(low, high):
            fn(i)
    else:
        lax.fori_loop(low, high, lambda i, c: (fn(i), c)[1], 0)


def kernel(
    ns, ng, nh,
    it_ref, res_ref, dir_ref, rho_ref, diag_ref, low_ref, up_ref, idx_ref, jac_ref, inv_ref, lf_ref, uf_ref,
    out_it, out_res, out_dir, out_rho,
    dfull, rfull, diagf, lowf, upf, jacf, invf, lff, uff,
    mh, ml, ih, il,
    face_out, face_in, tu, offs, fps, fback,
    sbuf, sums, rows_out, rows_in,
    m_send, m_recv, f_send, f_recv, t_send, t_recv, s_send, s_recv, r_send, r_recv,
):
    k = lax.axis_index("slab")
    g = lax.axis_index("grp")
    h = lax.rem(g, nh)
    base = g - h
    gb = dir_ref.shape[0]
    B = gb * ng
    IF = idx_ref.shape[1]

    def dev(slab, grp):
        return {"slab": slab, "grp": grp}

    def signal_slab(off):
        for j in range(nh):
            pl.semaphore_signal(bar, inc=1, device_id=dev(lax.rem(k + off, ns), base + j), device_id_type=MESH)

    bar = pltpu.get_barrier_semaphore()
    for off in range(1, ng):
        pl.semaphore_signal(bar, inc=1, device_id=dev(k, lax.rem(g + off, ng)), device_id_type=MESH)
    each(1, ns, signal_slab)
    pl.semaphore_wait(bar, (ng - 1) + (ns - 1) * nh)

    mine = pl.ds(pl.multiple_of(g * gb, 8), gb)

    mats = [
        (dir_ref, dfull), (diag_ref, diagf), (res_ref, rfull), (jac_ref, jacf), (low_ref, lowf), (up_ref, upf),
        (inv_ref, invf), (lf_ref, lff), (uf_ref, uff),
    ]
    D, DIAG, RES, JAC, LOW, UP, INV, LF, UF = range(9)

    def mat_copy(m, off):
        ref, full = mats[m]
        peer = lax.rem(g + off, ng)
        if m in (D, RES):
            src = ref.at[:, pl.ds(pl.multiple_of(lax.rem(peer, nh) * LANES, LANES), LANES)]
        else:
            src = ref
        return pltpu.make_async_remote_copy(
            src_ref=src, dst_ref=full.at[mine, :], send_sem=m_send.at[m, off], recv_sem=m_recv.at[m, off],
            device_id=dev(k, peer), device_id_type=MESH)

    for m in range(len(mats)):
        for off in range(1, ng):
            mat_copy(m, off).start()

    half = pl.ds(pl.multiple_of(h * LANES, LANES), LANES)
    dfull[mine, :] = dir_ref[:, half]
    rfull[mine, :] = res_ref[:, half]
    for m in range(len(mats)):
        if m not in (D, RES):
            mats[m][1][mine, :] = mats[m][0][...]

    def arrived(m):
        for off in range(1, ng):
            mat_copy(m, off).wait_recv()

    sel = jnp.transpose(
        (lax.broadcasted_iota(jnp.int32, (B, IF), 0) == idx_ref[...]).astype(F32)).astype(BF)

    def face_copy(slot, side):
        to = k + 1 if side == 0 else k - 1
        return pltpu.make_async_remote_copy(
            src_ref=face_out.at[slot], dst_ref=face_in.at[slot, side], send_sem=f_send.at[slot, side],
            recv_sem=f_recv.at[slot, side], device_id=dev(to, g), device_id_type=MESH)

    def send_face(slot, value):
        face_out[slot] = value

        @pl.when(k < ns - 1)
        def _():
            face_copy(slot, 0).start()

        @pl.when(k > 0)
        def _():
            face_copy(slot, 1).start()

    def wait_face(slot):
        @pl.when(k > 0)
        def _():
            face_copy(slot, 0).wait_recv()

        @pl.when(k < ns - 1)
        def _():
            face_copy(slot, 1).wait_recv()

    @pl.when(k == 0)
    def _():
        for slot in range(3):
            face_in[slot, 0] = jnp.zeros((IF, LANES), F32)

    @pl.when(k == ns - 1)
    def _():
        for slot in range(3):
            face_in[slot, 1] = jnp.zeros((IF, LANES), F32)

    def jacobi(field):
        return jnp.concatenate(
            [mm(*split(jacf[j * gb:(j + 1) * gb, :]), field[j * gb:(j + 1) * gb, :]) for j in range(ng)], axis=0)

    arrived(D)
    d = dfull[...]
    send_face(0, pick(sel, d))
    arrived(DIAG)
    mh[:, :B], ml[:, :B] = split(diagf[...])
    arrived(RES)
    arrived(JAC)
    r = rfull[...]
    jr = jacobi(r)
    send_face(1, pick(sel, jr))
    image = mm(mh[:, :B], ml[:, :B], d)
    arrived(LOW)
    mh[:, B:B + IF], ml[:, B:B + IF] = split(lowf[...])
    arrived(UP)
    mh[:, B + IF:], ml[:, B + IF:] = split(upf[...])
    wait_face(0)
    image = image + mm(mh[:, B:], ml[:, B:], jnp.concatenate([face_in[0, 0], face_in[0, 1]], axis=0))

    def sum_copy(which, off, j):
        to = lax.rem(k + off, ns)
        flat = off * nh + lax.rem(j + nh - h, nh)
        return pltpu.make_async_remote_copy(
            src_ref=sbuf.at[which], dst_ref=sums.at[which, k * nh + h], send_sem=s_send.at[which, flat],
            recv_sem=s_recv.at[which, flat], device_id=dev(to, base + j), device_id_type=MESH)

    def sum_desc(which, off, turn):
        flat = off * nh + turn
        frm_k = lax.rem(k + ns - off, ns)
        frm_h = lax.rem(h + nh - turn, nh)
        return pltpu.make_async_remote_copy(
            src_ref=sbuf.at[which], dst_ref=sums.at[which, frm_k * nh + frm_h], send_sem=s_send.at[which, flat],
            recv_sem=s_recv.at[which, flat], device_id=dev(lax.rem(k + off, ns), base + lax.rem(h + turn, nh)),
            device_id_type=MESH)

    def sum_send(which, value):
        sbuf[which] = value
        sums[which, k * nh + h] = value

        def go(off):
            for turn in range(nh):
                if isinstance(off, int) and off == 0 and turn == 0:
                    continue
                flat = off * nh + turn
                pltpu.make_async_remote_copy(
                    src_ref=sbuf.at[which], dst_ref=sums.at[which, k * nh + h], send_sem=s_send.at[which, flat],
                    recv_sem=s_recv.at[which, flat],
                    device_id=dev(lax.rem(k + off, ns), base + lax.rem(h + turn, nh)), device_id_type=MESH).start()

        go(0)
        each(1, ns, go)

    def sum_wait(which, turn):
        if turn != 0:
            sum_desc(which, 0, turn).wait_recv()
        each(1, ns, lambda off: sum_desc(which, off, turn).wait_recv())

    def total(which, j):
        return lax.fori_loop(
            0, ns, lambda i, acc: acc + sums[which, i * nh + j], jnp.zeros((1, LANES), F32))

    sum_send(0, jnp.sum(d * image, axis=0, keepdims=True))
    jim = jacobi(image)
    send_face(2, pick(sel, jim))

    def tu_copy(which, off):
        return pltpu.make_async_remote_copy(
            src_ref=tu.at[which, k], dst_ref=tu.at[which, k], send_sem=t_send.at[which, off],
            recv_sem=t_recv.at[which, off], device_id=dev(lax.rem(k + off, ns), g), device_id_type=MESH)

    def tu_wait(which, off):
        frm = lax.rem(k + ns - off, ns)
        pltpu.make_async_remote_copy(
            src_ref=tu.at[which, frm], dst_ref=tu.at[which, frm], send_sem=t_send.at[which, off],
            recv_sem=t_recv.at[which, off], device_id=dev(lax.rem(k + off, ns), g),
            device_id_type=MESH).wait_recv()

    arrived(INV)
    ih[:B, :], il[:B, :] = split(invf[...])
    ih[B:, :] = dot(sel, ih[:B, :]).astype(BF)
    il[B:, :] = dot(sel, il[:B, :]).astype(BF)
    arrived(LF)
    factor = mm(ih[...], il[...], lff[...])
    tu[0, k] = -factor[B:, :]
    each(1, ns, lambda off: tu_copy(0, off).start())
    fback[:, :IF] = factor[:B, :]
    arrived(UF)
    tu[1, k] = -pick(sel, uff[...])
    each(1, ns, lambda off: tu_copy(1, off).start())
    fback[:, IF:] = uff[...]

    rho = rho_ref[0:1, half]
    sum_wait(0, 0)
    alpha = rho / total(0, h)
    rn = r - alpha * image

    def rows_copy(which, turn):
        to = base + lax.rem(h + turn, nh)
        return pltpu.make_async_remote_copy(
            src_ref=rows_out.at[which, pl.ds(pl.multiple_of(to * gb, 8), gb), :], dst_ref=rows_in.at[which, turn],
            send_sem=r_send.at[which, turn], recv_sem=r_recv.at[which, turn], device_id=dev(k, to),
            device_id_type=MESH)

    rows_out[0] = rn
    for turn in range(1, nh):
        rows_copy(0, turn).start()
    wait_face(1)
    wait_face(2)
    s = jr - alpha * jim
    faces = jnp.concatenate(
        [s] + [face_in[1, side] - alpha * face_in[2, side] for side in range(2)], axis=0)
    defect = rn - mm(mh[...], ml[...], faces)
    both = mm(ih[...], il[...], defect)
    solved = both[:B, :]
    tu[2, k] = both[B:, :]
    each(1, ns, lambda off: tu_copy(2, off).start())

    for which in range(3):
        each(1, ns, functools.partial(tu_wait, which))

    def forward(i, prev):
        fps[i] = prev
        return tu[2, i] + mm(*split(tu[0, i]), prev)

    last = lax.fori_loop(0, ns, forward, jnp.zeros((IF, LANES), F32), unroll=ns <= 8)
    fps[ns] = last

    def backward(t, nxt):
        i = ns - 1 - t
        offs[i] = nxt
        return fps[i + 1] + mm(*split(tu[1, i]), nxt)

    lax.fori_loop(0, ns, backward, jnp.zeros((IF, LANES), F32), unroll=ns <= 8)
    ends = jnp.concatenate([fps[k], offs[k]], axis=0)
    precond = s + (solved - mm(*split(fback[...]), ends))
    rows_out[1] = precond
    for turn in range(1, nh):
        rows_copy(1, turn).start()
    sum_send(1, jnp.sum(rn * precond, axis=0, keepdims=True))

    def put(j_half, alpha_j, res_rows, turn):
        cols = pl.ds(pl.multiple_of(j_half * LANES, LANES), LANES)
        out_it[:, cols] = it_ref[:, cols] + alpha_j * dir_ref[:, cols]
        out_res[:, cols] = res_rows

    put(h, alpha, rows_out[0, mine, :], 0)
    for turn in range(1, nh):
        sum_wait(0, turn)
        j = lax.rem(h + nh - turn, nh)
        rows_copy(0, turn).wait_recv()
        cols = pl.ds(pl.multiple_of(j * LANES, LANES), LANES)
        put(j, rho_ref[0:1, cols] / total(0, j), rows_in[0, turn], turn)

    for turn in range(nh):
        sum_wait(1, turn)
        j = lax.rem(h + nh - turn, nh)
        cols = pl.ds(pl.multiple_of(j * LANES, LANES), LANES)
        new = total(1, j)
        out_rho[0:1, cols] = new
        if turn:
            rows_copy(1, turn).wait_recv()
            part = rows_in[1, turn]
        else:
            part = rows_out[1, mine, :]
        out_dir[:, cols] = part + new / rho_ref[0:1, cols] * dir_ref[:, cols]

    for m in range(len(mats)):
        for off in range(1, ng):
            mat_copy(m, off).wait_send()
    for slot in range(3):
        @pl.when(k < ns - 1)
        def _():
            face_copy(slot, 0).wait_send()

        @pl.when(k > 0)
        def _():
            face_copy(slot, 1).wait_send()
    for which in range(3):
        each(1, ns, lambda off: tu_copy(which, off).wait_send())
    for which in range(2):
        for turn in range(1, nh):
            rows_copy(which, turn).wait_send()
            sum_desc(which, 0, turn).wait_send()
        for turn in range(nh):
            each(1, ns, lambda off: sum_desc(which, off, turn).wait_send())


def local(ns, ng, iterate, residual, direction, prior_rho, *rest):
    gb, cols = direction.shape
    nh = cols // LANES
    B = gb * ng
    IF = rest[1].shape[1]
    row = jax.ShapeDtypeStruct((gb, cols), F32)
    V = pltpu.VMEM
    DMA = pltpu.SemaphoreType.DMA
    vm = pl.BlockSpec(memory_space=pltpu.VMEM)
    out = pl.pallas_call(
        functools.partial(kernel, ns, ng, nh),
        out_shape=(row, row, row, jax.ShapeDtypeStruct((1, cols), F32)),
        in_specs=[vm] * 12,
        out_specs=(vm,) * 4,
        scratch_shapes=[
            V((B, LANES), F32), V((B, LANES), F32), V((B, B), F32), V((B, IF), F32), V((B, IF), F32),
            V((B, gb), F32), V((B, B), F32), V((B, IF), F32), V((B, IF), F32),
            V((B, B + 2 * IF), BF), V((B, B + 2 * IF), BF), V((B + IF, B), BF), V((B + IF, B), BF),
            V((3, IF, LANES), F32), V((3, 2, IF, LANES), F32), V((3, ns, IF, LANES), F32),
            V((ns, IF, LANES), F32), V((ns + 1, IF, LANES), F32), V((B, 2 * IF), F32),
            V((2, 1, LANES), F32), V((2, ns * nh, 1, LANES), F32),
            V((2, B, LANES), F32), V((2, nh, gb, LANES), F32),
            DMA((9, ng)), DMA((9, ng)), DMA((3, 2)), DMA((3, 2)), DMA((3, ns)), DMA((3, ns)),
            DMA((2, ns * nh)), DMA((2, ns * nh)), DMA((2, nh)), DMA((2, nh)),
        ],
        compiler_params=pltpu.CompilerParams(
            collective_id=0, has_side_effects=True, vmem_limit_bytes=60 * 1024 * 1024),
    )(iterate, residual, direction, prior_rho.reshape(1, cols), *rest)
    return out[0], out[1], out[2], out[3].reshape(cols)


def solution(mesh):
    rows = P(("slab", "grp"), None)
    in_specs = (rows, rows, rows, P(), rows, rows, rows, P("slab", None), rows, rows, rows, rows)
    out_specs = (rows, rows, rows, P())
    body = functools.partial(local, mesh.shape["slab"], mesh.shape["grp"])
    return jax.shard_map(body, mesh=mesh, in_specs=in_specs, out_specs=out_specs, check_vma=False)
```

time: 255 us -> 85.2 us (0.33)
  blocking collectives: 193 us -> 0 us
  Pallas kernels: 0 us -> 80.6 us
  waiting for transfers between devices: 15.4 us -> 0 us
  between operations: 14.3 us -> 0.66 us
  matrix products: 12.2 us -> 0 us
  starting transfers between devices: 9.29 us -> 0 us
  local copies, waits for them, and re-layouts: 8.05 us -> 3.71 us
    all_gather x9 -> x0, blocking collectives: 115 us -> none  [the longest x2 69.6 us: prefix(): gathered = jax.tree.map(lambda a: lax.all_gather(a, axis), part)]
    pallas_call x0 -> x1, Pallas kernels: none -> 80.6 us  [local(): pl.pallas_call(functools.partial(kernel, ns, ng, nh), out_shape=(row, row...]
    psum x2 -> x0, blocking collectives: 78 us -> none  [the longest x1 41.1 us: local(): curvature = lax.psum(jnp.sum(direction * image, axis=0), ('slab', 'grp'))]
    dot_general x19 -> x0, matrix products: 12.2 us -> none  [matmul(): jnp.dot(left, right, precision=lax.Precision.HIGHEST, preferred_element_t...]
    ppermute x4 -> x0, waiting for transfers between devices: 10.8 us -> none  [the longest x2 7.72 us: extended(): lax.ppermute(head, axis, [((i + 1) % count, i) for i in range(ends)])]
    ppermute x4 -> x0, starting transfers between devices: 9.21 us -> none  [the longest x2 6.62 us: extended(): lax.ppermute(tail, axis, [(i, (i + 1) % count) for i in range(ends)])]
    all_gather x2 -> x0, waiting for transfers between devices: 4.55 us -> none  [prefix(): gathered = jax.tree.map(lambda a: lax.all_gather(a, axis), part)]
    gather x5 -> x0, local copies, waits for them, and re-layouts: 4.19 us -> none  [the longest x2 1.51 us: operate(): faces = gathered[index_rows]]
  transfers between devices with their start and end apart: 6 -> 0, of which waited for: 5 -> 0; matrix products, arithmetic and copies ran while one was open for 1% -> 0% of each run, Pallas kernels for 0% -> 0%
where the time goes in v1:
time: 85.2 us; the launch traced here: 85 us
  Pallas kernels  80.6 us (95%)
  local copies, waits for them, and re-layouts  3.71 us (4%)
    pallas_call x1, Pallas kernels, local(): pl.pallas_call(functools.partial(kernel, ns, ng, nh), out_shape=(row, row...  80.6 us
    unnamed x10, local copies, waits for them, and re-layouts  3.71 us

profile of v1, /device:TPU:0, one launch (start us, length us, event | category | flops | bytes accessed | tf_op | source)
XLA Modules:
  0.0 85.0 jit_solution(10704132769688071692)
XLA Ops:
  0.6 80.6 %shard_map.147 = (f32[96,256]{1,0:T(8,128)}, f32[96,256]{1,0:T(8,128)}, f32[96,256]{1,0:T(8,128)}, f32[1,256]{1,0:T(1,128)}) custom-call(f32[96,256]{1,0:T(8,128)} %it_ref.1, f32[96,256]{1,0:T(8,128)} %res_ref.1, f32[96,256]{1,0:T(8,128)} %dir_ref.1, f32[1,256]{1,0:T(1,128)} %bitcast.2, f32[96,384]{1,0:T(8,128)} %diag_ref.1, f32[96,128]{1,0:T(8,128)} %low_ref.1, ...), custom_call_target="tpu_custom_call" | custom-call | tf_op jit(solution)/shard_map/pallas_call | solution.py:350
  81.2 0.0 copy-start.1
  81.2 1.6 %copy.20 = f32[96,256]{1,0:T(8,128)} copy(f32[96,256]{1,0:T(8,128)} %get-tuple-element.16) | data formatting | bytes 196608
  82.8 0.0 copy-done.1
  82.8 0.0 copy-start
  82.8 0.6 copy.21
  83.5 0.3 copy-done
  83.7 0.0 copy-start.2
  83.7 0.6 copy.22
  84.4 0.0 copy-done.2
  84.4 0.6 copy.23
Async XLA Ops:
  81.2 1.6 %copy-start.1 = (f32[96,256]{1,0:T(8,128)S(1)}, f32[96,256]{1,0:T(8,128)}, u32[]{:S(2)}) copy-start(f32[96,256]{1,0:T(8,128)} %get-tuple-element.17) | copy-start | bytes 294916
  82.8 0.9 %copy-start = (f32[96,256]{1,0:T(8,128)S(1)}, f32[96,256]{1,0:T(8,128)}, u32[]{:S(2)}) copy-start(f32[96,256]{1,0:T(8,128)} %get-tuple-element.18) | copy-start | bytes 294916
  83.7 0.6 copy-start.2

commit v2 on v1

--- a/solution.py
+++ b/solution.py
@@ -50,9 +50,9 @@
     out_it, out_res, out_dir, out_rho,
     dfull, rfull, diagf, lowf, upf, jacf, invf, lff, uff,
     mh, ml, ih, il,
-    face_out, face_in, tu, offs, fps, fback,
+    face_out, face_in, tu, offs, fps, fback, fown, ffull,
     sbuf, sums, rows_out, rows_in,
-    m_send, m_recv, f_send, f_recv, t_send, t_recv, s_send, s_recv, r_send, r_recv,
+    m_send, m_recv, f_send, f_recv, t_send, t_recv, s_send, s_recv, r_send, r_recv, x_send, x_recv,
 ):
     k = lax.axis_index("slab")
     g = lax.axis_index("grp")
@@ -79,35 +79,53 @@
 
     mats = [
         (dir_ref, dfull), (diag_ref, diagf), (res_ref, rfull), (jac_ref, jacf), (low_ref, lowf), (up_ref, upf),
-        (inv_ref, invf), (lf_ref, lff), (uf_ref, uff),
+        (inv_ref, invf), (lf_ref, lff), (uf_ref, uff), (fown, ffull),
     ]
-    D, DIAG, RES, JAC, LOW, UP, INV, LF, UF = range(9)
-
-    def mat_copy(m, off):
+    D, DIAG, RES, JAC, LOW, UP, INV, LF, UF, FAC = range(10)
+
+    def mat_copy(m, flat):
         ref, full = mats[m]
-        peer = lax.rem(g + off, ng)
+        away, turn = flat // nh, flat % nh
         if m in (D, RES):
-            src = ref.at[:, pl.ds(pl.multiple_of(lax.rem(peer, nh) * LANES, LANES), LANES)]
+            peer = lax.rem(g + flat, ng)
+            src, dst = ref.at[:, pl.ds(pl.multiple_of(lax.rem(peer, nh) * LANES, LANES), LANES)], mine
+        elif turn == 0:
+            peer = lax.rem(g + away * nh, ng)
+            src, dst = ref, mine
         else:
-            src = ref
-        return pltpu.make_async_remote_copy(
-            src_ref=src, dst_ref=full.at[mine, :], send_sem=m_send.at[m, off], recv_sem=m_recv.at[m, off],
+            peer = base + lax.rem(h + turn, nh)
+            owner = lax.rem(g + ng - away * nh, ng)
+            dst = pl.ds(pl.multiple_of(owner * gb, 8), gb)
+            src = ref if away == 0 else full.at[dst, :]
+        return pltpu.make_async_remote_copy(
+            src_ref=src, dst_ref=full.at[dst, :], send_sem=m_send.at[m, flat], recv_sem=m_recv.at[m, flat],
             device_id=dev(k, peer), device_id_type=MESH)
 
-    for m in range(len(mats)):
-        for off in range(1, ng):
-            mat_copy(m, off).start()
+    def start(m):
+        for flat in range(1, ng):
+            if m in (D, RES) or flat < nh or flat % nh == 0:
+                mat_copy(m, flat).start()
+
+    for m in (LF, D, UF):
+        start(m)
+
+    def hand_on(m):
+        for away in range(1, ng // nh):
+            mat_copy(m, away * nh).wait_recv()
+            for turn in range(1, nh):
+                mat_copy(m, away * nh + turn).start()
 
     half = pl.ds(pl.multiple_of(h * LANES, LANES), LANES)
     dfull[mine, :] = dir_ref[:, half]
     rfull[mine, :] = res_ref[:, half]
     for m in range(len(mats)):
-        if m not in (D, RES):
+        if m not in (D, RES, FAC):
             mats[m][1][mine, :] = mats[m][0][...]
 
     def arrived(m):
-        for off in range(1, ng):
-            mat_copy(m, off).wait_recv()
+        for flat in range(1, ng):
+            if m in (D, RES) or flat < nh or flat % nh:
+                mat_copy(m, flat).wait_recv()
 
     sel = jnp.transpose(
         (lax.broadcasted_iota(jnp.int32, (B, IF), 0) == idx_ref[...]).astype(F32)).astype(BF)
@@ -152,16 +170,67 @@
         return jnp.concatenate(
             [mm(*split(jacf[j * gb:(j + 1) * gb, :]), field[j * gb:(j + 1) * gb, :]) for j in range(ng)], axis=0)
 
+    share = IF // nh
+    own_share = pl.ds(pl.multiple_of(h * share, 8), share)
+
+    nb = ng // nh
+    g_share = IF // nb
+    group_share = pl.ds(pl.multiple_of(g // nh * g_share, 8), g_share)
+    passes = (nh, nh, nb)
+
+    def tu_at(which, slab):
+        return tu.at[which, slab, group_share if which == 2 else own_share, :]
+
+    def tu_copy(which, off):
+        return pltpu.make_async_remote_copy(
+            src_ref=tu_at(which, k), dst_ref=tu_at(which, k), send_sem=t_send.at[which, off],
+            recv_sem=t_recv.at[which, off], device_id=dev(lax.rem(k + off, ns), g), device_id_type=MESH)
+
+    def tu_wait(which, off):
+        frm = lax.rem(k + ns - off, ns)
+        pltpu.make_async_remote_copy(
+            src_ref=tu_at(which, frm), dst_ref=tu_at(which, frm), send_sem=t_send.at[which, off],
+            recv_sem=t_recv.at[which, off], device_id=dev(lax.rem(k + off, ns), g),
+            device_id_type=MESH).wait_recv()
+
+    def tu_pass(which, turn, off):
+        to = lax.rem(g + turn * nh, ng) if which == 2 else base + lax.rem(h + turn, nh)
+        frm = lax.rem(k + ns - off, ns)
+        return pltpu.make_async_remote_copy(
+            src_ref=tu_at(which, frm), dst_ref=tu_at(which, frm), send_sem=x_send.at[which, turn, off],
+            recv_sem=x_recv.at[which, turn, off], device_id=dev(k, to), device_id_type=MESH)
+
+    def tu_hand_on(which, off):
+        tu_wait(which, off)
+        for turn in range(1, passes[which]):
+            tu_pass(which, turn, off).start()
+
+    hand_on(LF)
+    arrived(LF)
+    fown[...] = mm(*split(inv_ref[...]), lff[...])
+    ffull[mine, :] = fown[...]
+    for m in (FAC, DIAG, LOW, UP, RES, JAC, INV):
+        start(m)
+
     arrived(D)
     d = dfull[...]
     send_face(0, pick(sel, d))
+    hand_on(UF)
+    arrived(UF)
+    tu[1, k] = -pick(sel, uff[...])
+    each(1, ns, lambda off: tu_copy(1, off).start())
+    fback[:, IF:] = uff[...]
+    hand_on(FAC)
+    arrived(FAC)
+    tu[0, k] = -pick(sel, ffull[...])
+    each(1, ns, lambda off: tu_copy(0, off).start())
+    fback[:, :IF] = ffull[...]
+
+    hand_on(DIAG)
+    hand_on(LOW)
+    hand_on(UP)
     arrived(DIAG)
     mh[:, :B], ml[:, :B] = split(diagf[...])
-    arrived(RES)
-    arrived(JAC)
-    r = rfull[...]
-    jr = jacobi(r)
-    send_face(1, pick(sel, jr))
     image = mm(mh[:, :B], ml[:, :B], d)
     arrived(LOW)
     mh[:, B:B + IF], ml[:, B:B + IF] = split(lowf[...])
@@ -169,13 +238,6 @@
     mh[:, B + IF:], ml[:, B + IF:] = split(upf[...])
     wait_face(0)
     image = image + mm(mh[:, B:], ml[:, B:], jnp.concatenate([face_in[0, 0], face_in[0, 1]], axis=0))
-
-    def sum_copy(which, off, j):
-        to = lax.rem(k + off, ns)
-        flat = off * nh + lax.rem(j + nh - h, nh)
-        return pltpu.make_async_remote_copy(
-            src_ref=sbuf.at[which], dst_ref=sums.at[which, k * nh + h], send_sem=s_send.at[which, flat],
-            recv_sem=s_recv.at[which, flat], device_id=dev(to, base + j), device_id_type=MESH)
 
     def sum_desc(which, off, turn):
         flat = off * nh + turn
@@ -213,34 +275,20 @@
             0, ns, lambda i, acc: acc + sums[which, i * nh + j], jnp.zeros((1, LANES), F32))
 
     sum_send(0, jnp.sum(d * image, axis=0, keepdims=True))
-    jim = jacobi(image)
+    arrived(RES)
+    hand_on(JAC)
+    arrived(JAC)
+    r = rfull[...]
+    smooth = jacobi(jnp.concatenate([r, image], axis=1))
+    jr, jim = smooth[:, :LANES], smooth[:, LANES:]
+    send_face(1, pick(sel, jr))
     send_face(2, pick(sel, jim))
 
-    def tu_copy(which, off):
-        return pltpu.make_async_remote_copy(
-            src_ref=tu.at[which, k], dst_ref=tu.at[which, k], send_sem=t_send.at[which, off],
-            recv_sem=t_recv.at[which, off], device_id=dev(lax.rem(k + off, ns), g), device_id_type=MESH)
-
-    def tu_wait(which, off):
-        frm = lax.rem(k + ns - off, ns)
-        pltpu.make_async_remote_copy(
-            src_ref=tu.at[which, frm], dst_ref=tu.at[which, frm], send_sem=t_send.at[which, off],
-            recv_sem=t_recv.at[which, off], device_id=dev(lax.rem(k + off, ns), g),
-            device_id_type=MESH).wait_recv()
-
+    hand_on(INV)
     arrived(INV)
     ih[:B, :], il[:B, :] = split(invf[...])
     ih[B:, :] = dot(sel, ih[:B, :]).astype(BF)
     il[B:, :] = dot(sel, il[:B, :]).astype(BF)
-    arrived(LF)
-    factor = mm(ih[...], il[...], lff[...])
-    tu[0, k] = -factor[B:, :]
-    each(1, ns, lambda off: tu_copy(0, off).start())
-    fback[:, :IF] = factor[:B, :]
-    arrived(UF)
-    tu[1, k] = -pick(sel, uff[...])
-    each(1, ns, lambda off: tu_copy(1, off).start())
-    fback[:, IF:] = uff[...]
 
     rho = rho_ref[0:1, half]
     sum_wait(0, 0)
@@ -268,8 +316,12 @@
     tu[2, k] = both[B:, :]
     each(1, ns, lambda off: tu_copy(2, off).start())
 
+    for which in range(2):
+        each(1, ns, functools.partial(tu_hand_on, which))
+    each(1, ns, functools.partial(tu_hand_on, 2))
     for which in range(3):
-        each(1, ns, functools.partial(tu_wait, which))
+        for turn in range(1, passes[which]):
+            each(1, ns, lambda off: tu_pass(which, turn, off).wait_recv())
 
     def forward(i, prev):
         fps[i] = prev
@@ -330,6 +382,8 @@
             face_copy(slot, 1).wait_send()
     for which in range(3):
         each(1, ns, lambda off: tu_copy(which, off).wait_send())
+        for turn in range(1, passes[which]):
+            each(1, ns, lambda off: tu_pass(which, turn, off).wait_send())
     for which in range(2):
         for turn in range(1, nh):
             rows_copy(which, turn).wait_send()
@@ -357,11 +411,11 @@
             V((B, gb), F32), V((B, B), F32), V((B, IF), F32), V((B, IF), F32),
             V((B, B + 2 * IF), BF), V((B, B + 2 * IF), BF), V((B + IF, B), BF), V((B + IF, B), BF),
             V((3, IF, LANES), F32), V((3, 2, IF, LANES), F32), V((3, ns, IF, LANES), F32),
-            V((ns, IF, LANES), F32), V((ns + 1, IF, LANES), F32), V((B, 2 * IF), F32),
+            V((ns, IF, LANES), F32), V((ns + 1, IF, LANES), F32), V((B, 2 * IF), F32), V((gb, IF), F32), V((B, IF), F32),
             V((2, 1, LANES), F32), V((2, ns * nh, 1, LANES), F32),
             V((2, B, LANES), F32), V((2, nh, gb, LANES), F32),
-            DMA((9, ng)), DMA((9, ng)), DMA((3, 2)), DMA((3, 2)), DMA((3, ns)), DMA((3, ns)),
-            DMA((2, ns * nh)), DMA((2, ns * nh)), DMA((2, nh)), DMA((2, nh)),
+            DMA((10, ng)), DMA((10, ng)), DMA((3, 2)), DMA((3, 2)), DMA((3, ns)), DMA((3, ns)),
+            DMA((2, ns * nh)), DMA((2, ns * nh)), DMA((2, nh)), DMA((2, nh)), DMA((3, max(nh, ng // nh), ns)), DMA((3, max(nh, ng // nh), ns)),
         ],
         compiler_params=pltpu.CompilerParams(
             collective_id=0, has_side_effects=True, vmem_limit_bytes=60 * 1024 * 1024),

time: 85.2 us -> 59.8 us (0.70)
  Pallas kernels: 80.6 us -> 55.3 us
    pallas_call x1, Pallas kernels: 80.6 us -> 55.3 us  [local(): pl.pallas_call(functools.partial(kernel, ns, ng, nh), out_shape=(row, row...]
where the time goes in v2:
time: 59.8 us; the launch traced here: 59.6 us
  Pallas kernels  55.3 us (92%)
  local copies, waits for them, and re-layouts  3.71 us (6%)
  between operations  0.66 us (1%)
    pallas_call x1, Pallas kernels, local(): pl.pallas_call(functools.partial(kernel, ns, ng, nh), out_shape=(row, row...  55.3 us
    unnamed x10, local copies, waits for them, and re-layouts  3.71 us

profile of v2, /device:TPU:0, one launch (start us, length us, event | category | flops | bytes accessed | tf_op | source)
XLA Modules:
  0.0 59.6 jit_solution(13934707960268467885)
XLA Ops:
  0.6 55.3 %shard_map.147 = (f32[96,256]{1,0:T(8,128)}, f32[96,256]{1,0:T(8,128)}, f32[96,256]{1,0:T(8,128)}, f32[1,256]{1,0:T(1,128)}) custom-call(f32[96,256]{1,0:T(8,128)} %it_ref.1, f32[96,256]{1,0:T(8,128)} %res_ref.1, f32[96,256]{1,0:T(8,128)} %dir_ref.1, f32[1,256]{1,0:T(1,128)} %bitcast.2, f32[96,384]{1,0:T(8,128)} %diag_ref.1, f32[96,128]{1,0:T(8,128)} %low_ref.1, ...), custom_call_target="tpu_custom_call" | custom-call | tf_op jit(solution)/shard_map/pallas_call | solution.py:404
  55.9 0.0 copy-start.1
  55.9 1.6 %copy.20 = f32[96,256]{1,0:T(8,128)} copy(f32[96,256]{1,0:T(8,128)} %get-tuple-element.16) | data formatting | bytes 196608
  57.5 0.0 copy-done.1
  57.5 0.0 copy-start
  57.5 0.6 %copy.21 = f32[96,256]{1,0:T(8,128)} copy(f32[96,256]{1,0:T(8,128)S(1)} %copy-done.1) | data formatting | bytes 196608
  58.1 0.3 copy-done
  58.4 0.0 copy-start.2
  58.4 0.6 %copy.22 = f32[96,256]{1,0:T(8,128)} copy(f32[96,256]{1,0:T(8,128)S(1)} %copy-done) | data formatting | bytes 196608
  59.1 0.0 copy-done.2
  59.1 0.6 copy.23
Async XLA Ops:
  55.9 1.6 %copy-start.1 = (f32[96,256]{1,0:T(8,128)S(1)}, f32[96,256]{1,0:T(8,128)}, u32[]{:S(2)}) copy-start(f32[96,256]{1,0:T(8,128)} %get-tuple-element.17) | copy-start | bytes 294916
  57.5 0.9 %copy-start = (f32[96,256]{1,0:T(8,128)S(1)}, f32[96,256]{1,0:T(8,128)}, u32[]{:S(2)}) copy-start(f32[96,256]{1,0:T(8,128)} %get-tuple-element.18) | copy-start | bytes 294916
  58.4 0.6 %copy-start.2 = (f32[1,256]{1,0:T(1,128)S(1)}, f32[1,256]{1,0:T(1,128)}, u32[]{:S(2)}) copy-start(f32[1,256]{1,0:T(1,128)} %get-tuple-element.11) | copy-start | bytes 3076

commit v3 on v2

--- a/solution.py
+++ b/solution.py
@@ -46,11 +46,12 @@
 
 def kernel(
     ns, ng, nh,
-    it_ref, res_ref, dir_ref, rho_ref, diag_ref, low_ref, up_ref, idx_ref, jac_ref, inv_ref, lf_ref, uf_ref,
+    it_hbm, res_hbm, dir_hbm, rho_ref, diag_hbm, low_hbm, up_hbm, idx_ref, jac_hbm, inv_hbm, lf_hbm, uf_hbm,
     out_it, out_res, out_dir, out_rho,
     dfull, rfull, diagf, lowf, upf, jacf, invf, lff, uff,
     mh, ml, ih, il,
     face_out, face_in, tu, offs, fps, fback, fown, ffull,
+    it_ref, res_ref, dir_ref, diag_ref, low_ref, up_ref, jac_ref, inv_ref, lf_ref, uf_ref, in_sem,
     sbuf, sums, rows_out, rows_in,
     m_send, m_recv, f_send, f_recv, t_send, t_recv, s_send, s_recv, r_send, r_recv, x_send, x_recv,
 ):
@@ -73,6 +74,14 @@
     for off in range(1, ng):
         pl.semaphore_signal(bar, inc=1, device_id=dev(k, lax.rem(g + off, ng)), device_id_type=MESH)
     each(1, ns, signal_slab)
+    stage = [
+        pltpu.make_async_copy(src, dst, in_sem.at[i]) for i, (src, dst) in enumerate((
+            (lf_hbm, lf_ref), (dir_hbm, dir_ref), (uf_hbm, uf_ref), (inv_hbm, inv_ref), (diag_hbm, diag_ref),
+            (low_hbm, low_ref), (up_hbm, up_ref), (res_hbm, res_ref), (jac_hbm, jac_ref), (it_hbm, it_ref)))]
+    for copy in stage:
+        copy.start()
+    for copy in stage:
+        copy.wait()
     pl.semaphore_wait(bar, (ng - 1) + (ns - 1) * nh)
 
     mine = pl.ds(pl.multiple_of(g * gb, 8), gb)
@@ -318,7 +327,11 @@
 
     for which in range(2):
         each(1, ns, functools.partial(tu_hand_on, which))
-    each(1, ns, functools.partial(tu_hand_on, 2))
+    def nearest(i):
+        step = i // 2
+        return 1 + step + (i % 2) * (ns - 2 - 2 * step)
+
+    each(0, ns - 1, lambda i: tu_hand_on(2, nearest(i)))
     for which in range(3):
         for turn in range(1, passes[which]):
             each(1, ns, lambda off: tu_pass(which, turn, off).wait_recv())
@@ -404,7 +417,7 @@
     out = pl.pallas_call(
         functools.partial(kernel, ns, ng, nh),
         out_shape=(row, row, row, jax.ShapeDtypeStruct((1, cols), F32)),
-        in_specs=[vm] * 12,
+        in_specs=[vm if i in (3, 7) else pl.BlockSpec(memory_space=pl.ANY) for i in range(12)],
         out_specs=(vm,) * 4,
         scratch_shapes=[
             V((B, LANES), F32), V((B, LANES), F32), V((B, B), F32), V((B, IF), F32), V((B, IF), F32),
@@ -412,6 +425,7 @@
             V((B, B + 2 * IF), BF), V((B, B + 2 * IF), BF), V((B + IF, B), BF), V((B + IF, B), BF),
             V((3, IF, LANES), F32), V((3, 2, IF, LANES), F32), V((3, ns, IF, LANES), F32),
             V((ns, IF, LANES), F32), V((ns + 1, IF, LANES), F32), V((B, 2 * IF), F32), V((gb, IF), F32), V((B, IF), F32),
+            *[V(a.shape, F32) for a in (iterate, residual, direction, *rest[:1], *rest[1:3], *rest[4:])], DMA((10,)),
             V((2, 1, LANES), F32), V((2, ns * nh, 1, LANES), F32),
             V((2, B, LANES), F32), V((2, nh, gb, LANES), F32),
             DMA((10, ng)), DMA((10, ng)), DMA((3, 2)), DMA((3, 2)), DMA((3, ns)), DMA((3, ns)),

time: 59.8 us -> 58.8 us (0.983)
  Pallas kernels: 55.3 us -> 54.2 us
    pallas_call x1, Pallas kernels: 55.3 us -> 54.2 us  [local(): pl.pallas_call(functools.partial(kernel, ns, ng, nh), out_shape=(row, row...]
where the time goes in v3:
time: 58.8 us; the launch traced here: 58.5 us
  Pallas kernels  54.2 us (92%)
  local copies, waits for them, and re-layouts  3.71 us (6%)
  between operations  0.66 us (1%)
    pallas_call x1, Pallas kernels, local(): pl.pallas_call(functools.partial(kernel, ns, ng, nh), out_shape=(row, row...  54.2 us
    unnamed x10, local copies, waits for them, and re-layouts  3.71 us

profile of v3, /device:TPU:0, one launch (start us, length us, event | category | flops | bytes accessed | tf_op | source)
XLA Modules:
  0.0 58.5 jit_solution(15667356017540869998)
XLA Ops:
  0.6 54.2 %shard_map.147 = (f32[96,256]{1,0:T(8,128)}, f32[96,256]{1,0:T(8,128)}, f32[96,256]{1,0:T(8,128)}, f32[1,256]{1,0:T(1,128)}) custom-call(f32[96,256]{1,0:T(8,128)} %it_hbm.1, f32[96,256]{1,0:T(8,128)} %res_hbm.1, f32[96,256]{1,0:T(8,128)} %dir_hbm.1, f32[1,256]{1,0:T(1,128)} %bitcast.2, f32[96,384]{1,0:T(8,128)} %diag_hbm.1, f32[96,128]{1,0:T(8,128)} %low_hbm.1, ...), custom_call_target="tpu_custom_call" | custom-call | tf_op jit(solution)/shard_map/pallas_call | solution.py:417
  54.8 0.0 copy-start.1
  54.8 1.6 %copy.20 = f32[96,256]{1,0:T(8,128)} copy(f32[96,256]{1,0:T(8,128)} %get-tuple-element.16) | data formatting | bytes 196608
  56.4 0.0 copy-done.1
  56.4 0.0 copy-start
  56.4 0.6 %copy.21 = f32[96,256]{1,0:T(8,128)} copy(f32[96,256]{1,0:T(8,128)S(1)} %copy-done.1) | data formatting | bytes 196608
  57.0 0.3 copy-done
  57.3 0.0 copy-start.2
  57.3 0.6 %copy.22 = f32[96,256]{1,0:T(8,128)} copy(f32[96,256]{1,0:T(8,128)S(1)} %copy-done) | data formatting | bytes 196608
  58.0 0.0 copy-done.2
  58.0 0.6 copy.23
Async XLA Ops:
  54.8 1.6 %copy-start.1 = (f32[96,256]{1,0:T(8,128)S(1)}, f32[96,256]{1,0:T(8,128)}, u32[]{:S(2)}) copy-start(f32[96,256]{1,0:T(8,128)} %get-tuple-element.17) | copy-start | bytes 294916
  56.4 0.9 %copy-start = (f32[96,256]{1,0:T(8,128)S(1)}, f32[96,256]{1,0:T(8,128)}, u32[]{:S(2)}) copy-start(f32[96,256]{1,0:T(8,128)} %get-tuple-element.18) | copy-start | bytes 294916
  57.3 0.6 %copy-start.2 = (f32[1,256]{1,0:T(1,128)S(1)}, f32[1,256]{1,0:T(1,128)}, u32[]{:S(2)}) copy-start(f32[1,256]{1,0:T(1,128)} %get-tuple-element.11) | copy-start | bytes 3076
